TPU v7x, 128 devices: a whole 4x4x4 slice. The times are simulated.
128 devices in a mesh: ctx: 8 (over x, core), tp: 16 (over y, z).
Axes of the slice: x: 4, y: 4, z: 4, core: 2. Of those that a mesh axis runs over, the one named last changes fastest.
Arguments:
- streams: bfloat16 [3, 8192, 8192], P(None, 'ctx', 'tp'), may hold values from -6 to 6
- conv_weight: float32 [3, 3, 8192], P(None, None, 'tp'), may hold values from -3.5 to 3.5
- skip_weight: float32 [8192], P('tp'), may hold values from -4 to 4
- long_filter: bfloat16 [8192, 8192], P('ctx', 'tp'), may hold values from -1.6 to 1.6
- out_weight: bfloat16 [8192, 8192], P('tp'), may hold values from -0.09375 to 0.09375
Outputs:
- projected: bfloat16 [8192, 8192], P('ctx', 'tp')
All inputs are finite; a program needn't handle non-finite values.
Results may differ from a plain program's by a relative error of at most 0.015.
Values may be sent and summed in bfloat16 or wider, within the bound.
A program may use at most 128 MiB of HBM per device.

v0:
```python
import functools
import math

import jax
import jax.numpy as jnp
import ml_dtypes
import numpy as np
from jax import lax
from jax.experimental import pallas as pl
from jax.experimental.pallas import tpu as pltpu
from jax.sharding import PartitionSpec as P

BF = jnp.bfloat16
F32 = jnp.float32
MESH = pl.DeviceIdType.MESH

ROWS = 1024
CH = 512
CTX = 8
NY = 4
NZ = 4
LC = CH // CTX
TILES = ROWS // 128
NA = 64
GROUPS = LC // 4
NC = 8
CR = ROWS // NC


def tables():
    k1 = np.arange(64) + 0.25
    a = np.arange(64)
    b = np.arange(128)
    th1 = 2 * np.pi * np.outer(k1, a) / 64
    c1, s1 = np.cos(th1), np.sin(th1)
    eye = np.eye(4)
    f1 = np.concatenate([np.kron(eye, c1), np.kron(eye, s1)], axis=0)
    th2 = 2 * np.pi * np.outer(b, b) / 128
    c2, s2 = np.cos(th2), np.sin(th2)
    f2 = np.block([[c2, s2], [-s2, c2]])
    f2i = np.block([[c2, -s2], [s2, c2]])
    inv = np.concatenate([np.kron(eye, c1.T), np.kron(eye, s1.T)], axis=1) / 8192.0
    inv = inv.reshape(4, 8, 8, 512).transpose(1, 0, 2, 3).reshape(256, 512)
    tw = 2 * np.pi * np.outer(k1, b) / 8192
    twc, tws = np.tile(np.cos(tw), (4, 1)), np.tile(np.sin(tw), (4, 1))
    bf = lambda m: jnp.asarray(m.astype(np.float32).astype(ml_dtypes.bfloat16))
    return (
        bf(f1),
        bf(f2),
        bf(f2i),
        bf(inv),
        jnp.asarray(twc.astype(np.float32)),
        jnp.asarray(tws.astype(np.float32)),
        bf(np.eye(256)),
    )


def nt(a, b):
    return lax.dot_general(a, b, (((1,), (1,)), ((), ())), preferred_element_type=F32)


def mm(a, b):
    return jnp.dot(a, b, preferred_element_type=F32)


def kernel(
    x_ref, h_ref, cw_ref, skip_ref, w_ref, f1_ref, f2_ref, f2i_ref, f1i_ref, twc_ref, tws_ref, eye_ref,
    out_ref,
    halo, x32, gat, upos, sh, su, rh, ru, r32, spec, ys, ry, wr, gall, sopp, ra, rb, sl, sr, rl, rr, part,
    halo_sem, h_ss, h_rs, h_ls, u_ss, u_rs, u_ls, y_ss, y_rs, y_ls,
    w_ss, w_rs, w_ls, f_ss, f_rs, ag_ss, ag_rs, fw_ss, fw_rs, r1_ss, r1_rs, r2_ss, r2_rs,
):
    me = lax.axis_index("ctx")
    tp = lax.axis_index("tp")
    y = tp // NZ
    z = tp % NZ
    core = me % 2
    sib = me + 1 - 2 * core

    def dev(ctx, yy, zz):
        return (ctx, yy * NZ + zz)

    def remote(src, dst, ss, rs, to):
        return pltpu.make_async_remote_copy(
            src_ref=src, dst_ref=dst, send_sem=ss, recv_sem=rs, device_id=to, device_id_type=MESH
        )

    barrier = pltpu.get_barrier_semaphore()
    for d in range(1, CTX):
        pl.semaphore_signal(barrier, inc=1, device_id=dev((me + d) % CTX, y, z), device_id_type=MESH)
    for d in range(1, NZ):
        pl.semaphore_signal(barrier, inc=1, device_id=dev(me, y, (z + d) % NZ), device_id_type=MESH)
    for d in (1, 3):
        pl.semaphore_signal(barrier, inc=1, device_id=dev(me, (y + d) % NY, z), device_id_type=MESH)
    pl.semaphore_wait(barrier, 12)

    halo_cp = remote(
        x_ref.at[:, ROWS - 16 :, :], halo, halo_sem.at[0], halo_sem.at[1], dev((me + 1) % CTX, y, z)
    )
    halo_cp.start()

    half = pl.multiple_of(core * (CH // 2), CH // 2)
    w_cps = []
    for d in range(1, NZ):
        zp = (z + d) % NZ
        for yb in range(NY):
            cols = pl.multiple_of((NZ * yb + zp) * CH, CH)
            w_cps.append(
                remote(
                    w_ref.at[pl.ds(half, CH // 2), pl.ds(cols, CH)],
                    wr.at[yb, pl.ds(z * CH + half, CH // 2), :],
                    w_ss.at[d - 1, yb],
                    w_rs.at[d - 1, yb],
                    dev(me, y, zp),
                )
            )
    for cp in w_cps:
        cp.start()
    w_local = []
    for yb in range(NY):
        cols = pl.multiple_of((NZ * yb + z) * CH, CH)
        w_local.append(
            pltpu.make_async_copy(w_ref.at[:, pl.ds(cols, CH)], wr.at[yb, pl.ds(z * CH, CH), :], w_ls.at[yb])
        )
    for cp in w_local:
        cp.start()

    def exchange(send, recv, ss, rs, ls):
        cps = []
        for d in (4, 3, 5, 2, 6, 1, 7):
            j = (me + d) % CTX
            cps.append(
                remote(
                    send.at[:, pl.ds(pl.multiple_of(j * LC, LC), LC), :],
                    recv.at[pl.ds(me * TILES, TILES)],
                    ss.at[d - 1],
                    rs.at[d - 1],
                    dev(j, y, z),
                )
            )
        own = pltpu.make_async_copy(
            send.at[:, pl.ds(pl.multiple_of(me * LC, LC), LC), :], recv.at[pl.ds(me * TILES, TILES)], ls.at[0]
        )
        return cps, own

    eye = eye_ref[...]
    for t in range(TILES):
        for q in range(CH // 256):
            sh[t, 256 * q : 256 * q + 256, :] = nt(
                eye, h_ref[128 * t : 128 * t + 128, 256 * q : 256 * q + 256]
            ).astype(BF)
    h_cps, h_own = exchange(sh, rh, h_ss, h_rs, h_ls)
    for cp in h_cps:
        cp.start()
    h_own.start()

    for s in (1, 2, 0):
        x32[s, 8:, :] = x_ref[s].astype(F32)
    halo_cp.wait()
    edge = halo[...].astype(F32)[:, 8:16, :]
    x32[:, 0:8, :] = jnp.where(me == 0, jnp.zeros_like(edge), edge)

    def short(s, t, q):
        cs = slice(256 * q, 256 * q + 256)
        base = 8 + 128 * t
        acc = cw_ref[s, 0:1, cs] * x32[s, base : base + 128, cs]
        acc = acc + cw_ref[s, 1:2, cs] * x32[s, base - 1 : base + 127, cs]
        return acc + cw_ref[s, 2:3, cs] * x32[s, base - 2 : base + 126, cs]

    for t in range(TILES):
        for q in range(CH // 256):
            u = (short(1, t, q) * short(2, t, q)).astype(BF)
            upos[128 * t : 128 * t + 128, 256 * q : 256 * q + 256] = u
            su[t, 256 * q : 256 * q + 256, :] = nt(eye, u).astype(BF)
    u_cps, u_own = exchange(su, ru, u_ss, u_rs, u_ls)
    for cp in u_cps:
        cp.start()
    u_own.start()

    for t in range(TILES):
        for q in range(CH // 256):
            gat[128 * t : 128 * t + 128, 256 * q : 256 * q + 256] = short(0, t, q)

    def load_group(g):
        rows = [r32[pl.ds(4 * g + i, NA, stride=LC), :] for i in range(4)]
        return jnp.concatenate(rows, axis=0).astype(BF)

    def forward(v):
        o = mm(f1_ref[...], v)
        re, im = o[:256], o[256:]
        c, s = twc_ref[...], tws_ref[...]
        lhs = jnp.concatenate([(re * c - im * s).astype(BF), (re * s + im * c).astype(BF)], axis=1)
        return mm(lhs, f2_ref[...])

    for cp in h_cps:
        cp.wait()
    h_own.wait()
    r32[...] = rh[...].astype(F32).reshape(NA * LC, 128)

    def filter_group(g, carry):
        spec[g] = forward(load_group(g))
        return carry

    lax.fori_loop(0, GROUPS, filter_group, 0)

    for cp in u_cps:
        cp.wait()
    u_own.wait()
    r32[...] = ru[...].astype(F32).reshape(NA * LC, 128)

    def signal_group(g):
        o = forward(load_group(g))
        f = spec[g]
        ur, ui = o[:, :128], o[:, 128:]
        hr, hi = f[:, :128], f[:, 128:]
        lhs = jnp.concatenate([(ur * hr - ui * hi).astype(BF), (ur * hi + ui * hr).astype(BF)], axis=1)
        v = mm(lhs, f2i_ref[...])
        vr, vi = v[:, :128], v[:, 128:]
        c, s = twc_ref[...], tws_ref[...]
        return jnp.concatenate([(vr * c + vi * s).astype(BF), (vi * c - vr * s).astype(BF)], axis=0)

    def signal_pair(i, carry):
        v = jnp.concatenate([signal_group(2 * i), signal_group(2 * i + 1)], axis=1)
        o = mm(f1i_ref[...], v).astype(BF)
        for k in range(2):
            ys[:, pl.ds(pl.multiple_of(64 * i + 32 * k, 32), 32), :] = o[:, 128 * k : 128 * k + 128].reshape(8, 32, 128)
        return carry

    lax.fori_loop(0, GROUPS // 2, signal_pair, 0)

    y_cps = []
    for d in (4, 3, 5, 2, 6, 1, 7):
        j = (me + d) % CTX
        y_cps.append(remote(ys.at[j], ry.at[me], y_ss.at[d - 1], y_rs.at[d - 1], dev(j, y, z)))
    for cp in y_cps:
        cp.start()
    y_own = pltpu.make_async_copy(ys.at[me], ry.at[me], y_ls.at[0])
    y_own.start()

    f_cps = []
    for d in range(1, NZ):
        zs = (z + NZ - d) % NZ
        for yb in range(NY):
            w_cps[(d - 1) * NY + yb].wait()
            blk = wr.at[yb, pl.ds(zs * CH + half, CH // 2), :]
            cp = remote(blk, blk, f_ss.at[d - 1, yb], f_rs.at[d - 1, yb], dev(sib, y, z))
            cp.start()
            f_cps.append(cp)

    for cp in y_cps:
        cp.wait()
    y_own.wait()
    r32[...] = ry[...].astype(F32).reshape(CTX * 512, 128)
    eye128 = eye_ref[0:128, 0:128]
    for t in range(TILES):
        long_out = nt(eye128, r32[pl.ds(t, CH, stride=8), :].astype(BF))
        rows = slice(128 * t, 128 * t + 128)
        gated = (long_out + skip_ref[...] * upos[rows, :].astype(F32)) * gat[rows, :]
        gall[z, rows, :] = gated.astype(BF)

    for cp in w_local:
        cp.wait()
    for cp in f_cps:
        cp.wait()

    zl, zr, zo = (z + 3) % NZ, (z + 1) % NZ, (z + 2) % NZ
    yl, yr, yo = (y + 3) % NY, (y + 1) % NY, (y + 2) % NY
    hr_ = CR // 2
    ag, fw, r1, r2 = {}, {}, {}, {}
    for i in range(NC + 4):
        if i < NC:
            blk = gall.at[z, i * CR : (i + 1) * CR, :]
            ag[i] = (
                remote(blk, blk, ag_ss.at[0, i], ag_rs.at[0, i], dev(me, y, zr)),
                remote(blk, blk, ag_ss.at[1, i], ag_rs.at[1, i], dev(me, y, zl)),
            )
            for cp in ag[i]:
                cp.start()
        c = i - 1
        if 0 <= c < NC:
            up = gall.at[zl, c * CR : c * CR + hr_, :]
            dn = gall.at[zr, c * CR + hr_ : (c + 1) * CR, :]
            fw[c] = (
                remote(up, up, fw_ss.at[0, c], fw_rs.at[0, c], dev(me, y, zr)),
                remote(dn, dn, fw_ss.at[1, c], fw_rs.at[1, c], dev(me, y, zl)),
            )
            for k in range(2):
                ag[c][k].wait_recv()
                fw[c][k].start()
        c = i - 2
        if 0 <= c < NC:
            for k in range(2):
                fw[c][k].wait_recv()

            def product(yb):
                acc = mm(gall[0, c * CR : (c + 1) * CR, :], wr[yb, 0:CH, :])
                for k in range(1, NZ):
                    acc = acc + mm(gall[k, c * CR : (c + 1) * CR, :], wr[yb, k * CH : (k + 1) * CH, :])
                return acc

            sopp[c] = product(yo).astype(BF)
            r1[c] = (
                remote(sopp.at[c, 0:hr_, :], ra.at[c], r1_ss.at[0, c], r1_rs.at[0, c], dev(me, yr, z)),
                remote(sopp.at[c, hr_:CR, :], rb.at[c], r1_ss.at[1, c], r1_rs.at[1, c], dev(me, yl, z)),
            )
            for cp in r1[c]:
                cp.start()
            part[c % 3, 1] = product(yr)
            part[c % 3, 2] = product(yl)
            part[c % 3, 0] = product(y)
        c = i - 3
        if 0 <= c < NC:
            p = c % 3
            r1[c][0].wait_recv()
            sr[c, 0:hr_, :] = (part[p, 1, 0:hr_, :] + ra[c].astype(F32)).astype(BF)
            sr[c, hr_:CR, :] = part[p, 1, hr_:CR, :].astype(BF)
            r1[c][1].wait_recv()
            sl[c, hr_:CR, :] = (part[p, 2, hr_:CR, :] + rb[c].astype(F32)).astype(BF)
            sl[c, 0:hr_, :] = part[p, 2, 0:hr_, :].astype(BF)
            r2[c] = (
                remote(sr.at[c], rl.at[c], r2_ss.at[0, c], r2_rs.at[0, c], dev(me, yr, z)),
                remote(sl.at[c], rr.at[c], r2_ss.at[1, c], r2_rs.at[1, c], dev(me, yl, z)),
            )
            for cp in r2[c]:
                cp.start()
        c = i - 4
        if 0 <= c < NC:
            for cp in r2[c]:
                cp.wait_recv()
            total = part[c % 3, 0] + rl[c].astype(F32) + rr[c].astype(F32)
            out_ref[c * CR : (c + 1) * CR, :] = total.astype(BF)
    for c in range(NC):
        for cps in (ag[c], fw[c], r1[c], r2[c]):
            for cp in cps:
                cp.wait_send()


def on_device(streams, conv_weight, skip_weight, long_filter, out_weight):
    vm = pl.BlockSpec(memory_space=pltpu.VMEM)
    dma = pltpu.SemaphoreType.DMA
    return pl.pallas_call(
        kernel,
        out_shape=jax.ShapeDtypeStruct((ROWS, CH), BF),
        in_specs=[vm, vm, vm, vm, pl.BlockSpec(memory_space=pl.ANY)] + [vm] * 7,
        out_specs=vm,
        scratch_shapes=[
            pltpu.VMEM((3, 16, CH), BF),
            pltpu.VMEM((3, 8 + ROWS, CH), F32),
            pltpu.VMEM((ROWS, CH), F32),
            pltpu.VMEM((ROWS, CH), BF),
            pltpu.VMEM((TILES, CH, 128), BF),
            pltpu.VMEM((TILES, CH, 128), BF),
            pltpu.VMEM((NA, LC, 128), BF),
            pltpu.VMEM((NA, LC, 128), BF),
            pltpu.VMEM((NA * LC, 128), F32),
            pltpu.VMEM((GROUPS, 256, 256), F32),
            pltpu.VMEM((CTX, 512, 128), BF),
            pltpu.VMEM((CTX, 512, 128), BF),
            pltpu.VMEM((NY, NZ * CH, CH), BF),
            pltpu.VMEM((NZ, ROWS, CH), BF),
            pltpu.VMEM((NC, CR, CH), BF),
            pltpu.VMEM((NC, CR // 2, CH), BF),
            pltpu.VMEM((NC, CR // 2, CH), BF),
            pltpu.VMEM((NC, CR, CH), BF),
            pltpu.VMEM((NC, CR, CH), BF),
            pltpu.VMEM((NC, CR, CH), BF),
            pltpu.VMEM((NC, CR, CH), BF),
            pltpu.VMEM((3, 3, CR, CH), F32),
            dma((2,)),
            dma((7,)), dma((7,)), dma((1,)),
            dma((7,)), dma((7,)), dma((1,)),
            dma((7,)), dma((7,)), dma((1,)),
            dma((3, NY)), dma((3, NY)), dma((NY,)),
            dma((3, NY)), dma((3, NY)),
            dma((2, NC)), dma((2, NC)),
            dma((2, NC)), dma((2, NC)),
            dma((2, NC)), dma((2, NC)),
            dma((2, NC)), dma((2, NC)),
        ],
        compiler_params=pltpu.CompilerParams(
            collective_id=0, has_side_effects=True, vmem_limit_bytes=60 * 1024 * 1024
        ),
        name="hyena",
    )(streams, long_filter, conv_weight, skip_weight.reshape(1, CH), out_weight, *tables())


def solution(mesh):
    return jax.shard_map(
        on_device,
        mesh=mesh,
        in_specs=(
            P(None, "ctx", "tp"),
            P(None, None, "tp"),
            P("tp"),
            P("ctx", "tp"),
            P("tp", None),
        ),
        out_specs=P("ctx", "tp"),
        check_vma=False,
    )
```

profile of v0, /device:TPU:0, one launch (start us, length us, event | category | flops | bytes accessed | tf_op | source)
XLA Modules:
  0.0 116.3 jit_solution(4164259730869136699)
XLA Ops:
  0.0 114.1 %hyena.1 = bf16[1024,512]{1,0:T(8,128)(2,1)} custom-call(bf16[3,1024,512]{2,1,0:T(8,128)(2,1)} %x_ref.1, bf16[1024,512]{1,0:T(8,128)(2,1)} %h_ref.1, f32[3,3,512]{2,1,0:T(4,128)} %cw_ref.1, f32[1,512]{1,0:T(1,128)} %bitcast.1, bf16[512,8192]{1,0:T(8,128)(2,1)} %w_ref.1, bf16[512,256]{1,0:T(8,128)(2,1)} %constant.14.clone.f1_ref, ...), custom_call_target="tpu_custom_call" | custom-call | tf_op jit(solution)/shard_map/hyena/pallas_call | solution.py:341
  114.1 2.3 %copy.14 = bf16[1024,512]{1,0:T(8,128)(2,1)} copy(bf16[1024,512]{1,0:T(8,128)(2,1)} %hyena.1) | data formatting | bytes 2097152
where the time goes:
time: 116 us
  Pallas kernels  114 us (98%)
  local copies, waits for them, and re-layouts  2.26 us (2%)
    pallas_call x1, Pallas kernels, on_device(): pl.pallas_call(kernel, out_shape=jax.ShapeDtypeStruct((ROWS, CH), BF), in...  114 us

commit v1 on v0

v1 whole, which is shorter than its diff:
```python
import functools
import math

import jax
import jax.numpy as jnp
import ml_dtypes
import numpy as np
from jax import lax
from jax.experimental import pallas as pl
from jax.experimental.pallas import tpu as pltpu
from jax.sharding import PartitionSpec as P

BF = jnp.bfloat16
F32 = jnp.float32
MESH = pl.DeviceIdType.MESH

ROWS = 1024
CH = 512
CTX = 8
NY = 4
NZ = 4
LC = CH // CTX
LH = LC // 2
WQ = CH // 8
TILES = ROWS // 128
NA = 64
GROUPS = LC // 4
NC = 8
CR = ROWS // NC
ORDER = (
    *"goowgofgfgofvmmorfrmofemoefrmrofmerfmermereree",
)
QS = 4


def tables():
    k1 = np.arange(64) + 0.25
    a = np.arange(64)
    b = np.arange(128)
    th1 = 2 * np.pi * np.outer(k1, a) / 64
    c1, s1 = np.cos(th1), np.sin(th1)
    eye = np.eye(4)
    f1 = np.concatenate([np.kron(eye, c1), np.kron(eye, s1)], axis=0)
    th2 = 2 * np.pi * np.outer(b, b) / 128
    c2, s2 = np.cos(th2), np.sin(th2)
    f2 = np.block([[c2, s2], [-s2, c2]])
    f2i = np.block([[c2, -s2], [s2, c2]])
    inv = np.concatenate([np.kron(eye, c1.T), np.kron(eye, s1.T)], axis=1) / 8192.0
    inv = inv.reshape(4, 8, 4, 2, 512).transpose(2, 1, 0, 3, 4).reshape(256, 512)
    tw = 2 * np.pi * np.outer(k1, b) / 8192
    twc, tws = np.tile(np.cos(tw), (4, 1)), np.tile(np.sin(tw), (4, 1))
    bf = lambda m: jnp.asarray(m.astype(np.float32).astype(ml_dtypes.bfloat16))
    return (
        bf(f1),
        bf(f2),
        bf(f2i),
        bf(inv),
        jnp.asarray(twc.astype(np.float32)),
        jnp.asarray(tws.astype(np.float32)),
    )


def nt(a, b):
    return lax.dot_general(a, b, (((1,), (1,)), ((), ())), preferred_element_type=F32)


def mm(a, b):
    return jnp.dot(a, b, preferred_element_type=F32)


def kernel(
    x_ref, h_ref, cw_ref, skip_ref, w_ref, f1_ref, f2_ref, f2i_ref, f1i_ref, twc_ref, tws_ref,
    out_ref,
    xv, hv, tb1, tb2, tb3, tb4, tb5, tb6, outv, halo, x32, gat, upos, sh, su, rh, ru, r32, spec, ys, ry, wr, gall, sopp, ra, rb, sl, sr, rl, rr, part,
    in_sem, out_sem, halo_sem, h_ss, h_rs, h_ls, u_ss, u_rs, u_ls, y_ss, y_rs, y_ls,
    w_ss, w_rs, w_ls, f_ss, f_rs, x_ss, x_rs, ag_ss, ag_rs, fw_ss, fw_rs, r1_ss, r1_rs, r2_ss, r2_rs,
):
    me = lax.axis_index("ctx")
    tp = lax.axis_index("tp")
    y = tp // NZ
    z = tp % NZ
    core = me % 2
    sib = me + 1 - 2 * core

    def dev(ctx, yy, zz):
        return (ctx, yy * NZ + zz)

    def remote(src, dst, ss, rs, to):
        return pltpu.make_async_remote_copy(
            src_ref=src, dst_ref=dst, send_sem=ss, recv_sem=rs, device_id=to, device_id_type=MESH
        )

    ins = [
        pltpu.make_async_copy(src, dst, in_sem.at[k])
        for k, (src, dst) in enumerate(
            [(h_ref, hv), (x_ref.at[1], xv.at[1]), (x_ref.at[2], xv.at[2]), (x_ref.at[0], xv.at[0]),
             (f1_ref, tb1), (f2_ref, tb2), (f2i_ref, tb3), (f1i_ref, tb4), (twc_ref, tb5), (tws_ref, tb6)]
        )
    ]
    for cp in ins:
        cp.start()

    barrier = pltpu.get_barrier_semaphore()
    for d in range(1, CTX):
        pl.semaphore_signal(barrier, inc=1, device_id=dev((me + d) % CTX, y, z), device_id_type=MESH)
    for d in range(1, NZ):
        pl.semaphore_signal(barrier, inc=1, device_id=dev(me, y, (z + d) % NZ), device_id_type=MESH)
    for d in (1, 3):
        pl.semaphore_signal(barrier, inc=1, device_id=dev(me, (y + d) % NY, z), device_id_type=MESH)
    pl.semaphore_wait(barrier, 12)

    halo_cp = remote(
        x_ref.at[:, ROWS - 16 :, :], halo, halo_sem.at[0], halo_sem.at[1], dev((me + 1) % CTX, y, z)
    )
    halo_cp.start()

    half = pl.multiple_of(core * (CH // 2), CH // 2)
    w_cps = {}
    quarter = pl.multiple_of(half + (me // 2) * WQ, WQ)
    for d in (2, 1, 3):
        zp = (z + d) % NZ
        first, count = (quarter, WQ) if d == 2 else (half, CH // 2)
        for k in range(NY):
            yb = (y + k) % NY
            cols = pl.multiple_of((NZ * yb + zp) * CH, CH)
            w_cps[d, k] = remote(
                w_ref.at[pl.ds(first, count), pl.ds(cols, CH)],
                wr.at[yb, pl.ds(z * CH + first, count), :],
                w_ss.at[d - 1, k],
                w_rs.at[d - 1, k],
                dev(me, y, zp),
            )
    for cp in w_cps.values():
        cp.start()
    w_local = []
    for yb in range(NY):
        cols = pl.multiple_of((NZ * yb + z) * CH, CH)
        w_local.append(
            pltpu.make_async_copy(w_ref.at[:, pl.ds(cols, CH)], wr.at[yb, pl.ds(z * CH, CH), :], w_ls.at[yb])
        )
    for cp in w_local:
        cp.start()

    def exchange(send, recv, ss, rs, ls):
        both = []
        for h in range(2):
            cps = []
            for d in (4, 3, 5, 2, 6, 1, 7):
                j = (me + d) % CTX
                cps.append(
                    remote(
                        send.at[:, pl.ds(pl.multiple_of(j * LC + h * LH, LH), LH), :],
                        recv.at[h, pl.ds(me * TILES, TILES)],
                        ss.at[h, d - 1],
                        rs.at[h, d - 1],
                        dev(j, y, z),
                    )
                )
            cps.append(
                pltpu.make_async_copy(
                    send.at[:, pl.ds(pl.multiple_of(me * LC + h * LH, LH), LH), :],
                    recv.at[h, pl.ds(me * TILES, TILES)],
                    ls.at[h],
                )
            )
            both.append(cps)
        return both

    eye = (
        lax.broadcasted_iota(jnp.int32, (256, 256), 0) == lax.broadcasted_iota(jnp.int32, (256, 256), 1)
    ).astype(F32).astype(BF)
    ins[0].wait()
    for t in range(TILES):
        for q in range(CH // 256):
            sh[t, 256 * q : 256 * q + 256, :] = nt(
                eye, hv[128 * t : 128 * t + 128, 256 * q : 256 * q + 256]
            ).astype(BF)
    h_cps = exchange(sh, rh, h_ss, h_rs, h_ls)
    for cp in h_cps[0] + h_cps[1]:
        cp.start()

    for k, s in ((1, 1), (2, 2), (3, 0)):
        ins[k].wait()
        x32[s, 8:, :] = xv[s].astype(F32)
    halo_cp.wait()
    edge = halo[...].astype(F32)[:, 8:16, :]
    x32[:, 0:8, :] = jnp.where(me == 0, jnp.zeros_like(edge), edge)

    def short(s, t, q):
        cs = slice(256 * q, 256 * q + 256)
        base = 8 + 128 * t
        acc = cw_ref[s, 0:1, cs] * x32[s, base : base + 128, cs]
        acc = acc + cw_ref[s, 1:2, cs] * x32[s, base - 1 : base + 127, cs]
        return acc + cw_ref[s, 2:3, cs] * x32[s, base - 2 : base + 126, cs]

    for t in range(TILES):
        for q in range(CH // 256):
            u = (short(1, t, q) * short(2, t, q)).astype(BF)
            upos[128 * t : 128 * t + 128, 256 * q : 256 * q + 256] = u
            su[t, 256 * q : 256 * q + 256, :] = nt(eye, u).astype(BF)
    u_cps = exchange(su, ru, u_ss, u_rs, u_ls)
    for cp in u_cps[0] + u_cps[1]:
        cp.start()

    for t in range(TILES):
        for q in range(CH // 256):
            gat[128 * t : 128 * t + 128, 256 * q : 256 * q + 256] = short(0, t, q)

    for cp in ins[4:]:
        cp.wait()

    def load_group(h, g):
        rows = [r32[h, pl.ds(4 * g + i, NA, stride=LH), :] for i in range(4)]
        return jnp.concatenate(rows, axis=0).astype(BF)

    def forward(v):
        o = mm(tb1[...], v)
        re, im = o[:256], o[256:]
        c, s = tb5[...], tb6[...]
        lhs = jnp.concatenate([(re * c - im * s).astype(BF), (re * s + im * c).astype(BF)], axis=1)
        return mm(lhs, tb2[...])

    for h in range(2):
        for cp in h_cps[h]:
            cp.wait()
        r32[h] = rh[h].astype(F32).reshape(NA * LH, 128)

        def filter_group(g, carry, h=h):
            spec[h * (GROUPS // 2) + g] = forward(load_group(h, g))
            return carry

        lax.fori_loop(0, GROUPS // 2, filter_group, 0)

    opp = pl.multiple_of(((z + 2) % NZ) * CH + quarter, WQ)
    x_cps = {}

    def line(ks):
        for k in ks:
            blk = wr.at[(y + k) % NY, pl.ds(opp, WQ), :]
            w_cps[2, k].wait()
            for n in range(1, 4):
                to = dev((me + 2 * n) % CTX, y, z)
                x_cps[k, n] = remote(blk, blk, x_ss.at[k, n - 1], x_rs.at[k, n - 1], to)
                x_cps[k, n].start()

    def signal_group(h, g):
        o = forward(load_group(h, g))
        f = spec[h * (GROUPS // 2) + g]
        ur, ui = o[:, :128], o[:, 128:]
        hr, hi = f[:, :128], f[:, 128:]
        lhs = jnp.concatenate([(ur * hr - ui * hi).astype(BF), (ur * hi + ui * hr).astype(BF)], axis=1)
        v = mm(lhs, tb3[...])
        vr, vi = v[:, :128], v[:, 128:]
        c, s = tb5[...], tb6[...]
        return jnp.concatenate([(vr * c + vi * s).astype(BF), (vi * c - vr * s).astype(BF)], axis=0)

    for h in range(2):
        for cp in u_cps[h]:
            cp.wait()
        if h == 1:
            line((2, 1))
        r32[h] = ru[h].astype(F32).reshape(NA * LH, 128)

        def signal_pair(i, carry, h=h):
            v = jnp.concatenate([signal_group(h, 2 * i), signal_group(h, 2 * i + 1)], axis=1)
            o = mm(tb4[...], v)
            o = jnp.concatenate([o[:, :128].reshape(32, 8, 128), o[:, 128:].reshape(32, 8, 128)], axis=1)
            at = pl.multiple_of(16 * (h * (GROUPS // 4) + i), 16)
            ys[:, :, pl.ds(at, 16), :] = o.reshape(QS, CTX, 16, 128).astype(BF)
            return carry

        lax.fori_loop(0, GROUPS // 4, signal_pair, 0)

    y_cps = []
    for q in range(QS):
        cps = []
        for d in (4, 3, 5, 2, 6, 1, 7):
            j = (me + d) % CTX
            cps.append(remote(ys.at[q, j], ry.at[q, me], y_ss.at[q, d - 1], y_rs.at[q, d - 1], dev(j, y, z)))
        cps.append(pltpu.make_async_copy(ys.at[q, me], ry.at[q, me], y_ls.at[q]))
        for cp in cps:
            cp.start()
        if q == 0:
            line((3, 0))
        y_cps.append(cps)
    eye128 = eye[0:128, 0:128]

    def gate(q):
        for cp in y_cps[q]:
            cp.wait()
        r32[q // 2, 1024 * (q % 2) : 1024 * (q % 2) + 1024, :] = ry[q].astype(F32).reshape(1024, 128)
        for k in range(2):
            long_out = nt(eye128, r32[q // 2, pl.ds(1024 * (q % 2) + k, CH, stride=2), :].astype(BF))
            rows = slice(256 * q + 128 * k, 256 * q + 128 * k + 128)
            gated = (long_out + skip_ref[...] * upos[rows, :].astype(F32)) * gat[rows, :]
            gall[z, rows, :] = gated.astype(BF)

    f_cps = {}

    def share(d):
        blk = wr.at[:, pl.ds(pl.multiple_of(((z + NZ - d) % NZ) * CH + half, CH // 2), CH // 2), :]
        f_cps[d] = remote(blk, blk, f_ss.at[d - 1], f_rs.at[d - 1], dev(sib, y, z))
        f_cps[d].start()

    def weights(step):
        if step == 0:
            for d in (1, 3):
                for k in range(NY):
                    w_cps[d, k].wait()
                share(d)
        else:
            for cp in x_cps.values():
                cp.wait()
            share(2)
            for cp in w_local:
                cp.wait()
            for cp in f_cps.values():
                cp.wait()

    zl, zr, zo = (z + 3) % NZ, (z + 1) % NZ, (z + 2) % NZ
    yl, yr, yo = (y + 3) % NY, (y + 1) % NY, (y + 2) % NY
    hr_ = CR // 2
    ag, fw, r1, r2, oc = {}, {}, {}, {}, {}

    def own(c):
        blk = gall.at[z, c * CR : (c + 1) * CR, :]
        ag[c] = (
            remote(blk, blk, ag_ss.at[0, c], ag_rs.at[0, c], dev(me, y, zr)),
            remote(blk, blk, ag_ss.at[1, c], ag_rs.at[1, c], dev(me, y, zl)),
        )
        for cp in ag[c]:
            cp.start()

    def pass_on(c):
        up = gall.at[zl, c * CR : c * CR + hr_, :]
        dn = gall.at[zr, c * CR + hr_ : (c + 1) * CR, :]
        fw[c] = (
            remote(up, up, fw_ss.at[0, c], fw_rs.at[0, c], dev(me, y, zr)),
            remote(dn, dn, fw_ss.at[1, c], fw_rs.at[1, c], dev(me, y, zl)),
        )
        for k in range(2):
            ag[c][k].wait_recv()
            fw[c][k].start()

    def multiply(c):
        for k in range(2):
            fw[c][k].wait_recv()

        def product(yb):
            acc = mm(gall[0, c * CR : (c + 1) * CR, :], wr[yb, 0:CH, :])
            for k in range(1, NZ):
                acc = acc + mm(gall[k, c * CR : (c + 1) * CR, :], wr[yb, k * CH : (k + 1) * CH, :])
            return acc

        sopp[c] = product(yo).astype(BF)
        r1[c] = (
            remote(sopp.at[c, 0:hr_, :], ra.at[c], r1_ss.at[0, c], r1_rs.at[0, c], dev(me, yr, z)),
            remote(sopp.at[c, hr_:CR, :], rb.at[c], r1_ss.at[1, c], r1_rs.at[1, c], dev(me, yl, z)),
        )
        for cp in r1[c]:
            cp.start()
        part[c, 1] = product(yr)
        part[c, 2] = product(yl)
        part[c, 0] = product(y)

    def reduce(c):
        r1[c][0].wait_recv()
        sr[c, 0:hr_, :] = (part[c, 1, 0:hr_, :] + ra[c].astype(F32)).astype(BF)
        sr[c, hr_:CR, :] = part[c, 1, hr_:CR, :].astype(BF)
        r1[c][1].wait_recv()
        sl[c, hr_:CR, :] = (part[c, 2, hr_:CR, :] + rb[c].astype(F32)).astype(BF)
        sl[c, 0:hr_, :] = part[c, 2, 0:hr_, :].astype(BF)
        r2[c] = (
            remote(sr.at[c], rl.at[c], r2_ss.at[0, c], r2_rs.at[0, c], dev(me, yr, z)),
            remote(sl.at[c], rr.at[c], r2_ss.at[1, c], r2_rs.at[1, c], dev(me, yl, z)),
        )
        for cp in r2[c]:
            cp.start()

    def end(c):
        for cp in r2[c]:
            cp.wait_recv()
        total = part[c, 0] + rl[c].astype(F32) + rr[c].astype(F32)
        outv[c * CR : (c + 1) * CR, :] = total.astype(BF)
        oc[c] = pltpu.make_async_copy(
            outv.at[c * CR : (c + 1) * CR, :], out_ref.at[c * CR : (c + 1) * CR, :], out_sem.at[c]
        )
        oc[c].start()

    steps = dict(g=gate, o=own, f=pass_on, w=weights, m=multiply, r=reduce, e=end)
    count = dict.fromkeys(steps, 0)
    for k in ORDER:
        k = "w" if k == "v" else k
        steps[k](count[k])
        count[k] += 1
    for c in range(NC):
        for cps in (ag[c], fw[c], r1[c], r2[c]):
            for cp in cps:
                cp.wait_send()
        oc[c].wait()


def on_device(streams, conv_weight, skip_weight, long_filter, out_weight):
    vm = pl.BlockSpec(memory_space=pltpu.VMEM)
    hbm = pl.BlockSpec(memory_space=pl.ANY)
    dma = pltpu.SemaphoreType.DMA
    return pl.pallas_call(
        kernel,
        out_shape=jax.ShapeDtypeStruct((ROWS, CH), BF),
        in_specs=[hbm, hbm, vm, vm] + [hbm] * 7,
        out_specs=hbm,
        scratch_shapes=[
            pltpu.VMEM((3, ROWS, CH), BF),
            pltpu.VMEM((ROWS, CH), BF),
            pltpu.VMEM((512, 256), BF),
            pltpu.VMEM((256, 256), BF),
            pltpu.VMEM((256, 256), BF),
            pltpu.VMEM((256, 512), BF),
            pltpu.VMEM((256, 128), F32),
            pltpu.VMEM((256, 128), F32),
            pltpu.VMEM((ROWS, CH), BF),
            pltpu.VMEM((3, 16, CH), BF),
            pltpu.VMEM((3, 8 + ROWS, CH), F32),
            pltpu.VMEM((ROWS, CH), F32),
            pltpu.VMEM((ROWS, CH), BF),
            pltpu.VMEM((TILES, CH, 128), BF),
            pltpu.VMEM((TILES, CH, 128), BF),
            pltpu.VMEM((2, NA, LH, 128), BF),
            pltpu.VMEM((2, NA, LH, 128), BF),
            pltpu.VMEM((2, NA * LH, 128), F32),
            pltpu.VMEM((GROUPS, 256, 256), F32),
            pltpu.VMEM((QS, CTX, 128, 128), BF),
            pltpu.VMEM((QS, CTX, 128, 128), BF),
            pltpu.VMEM((NY, NZ * CH, CH), BF),
            pltpu.VMEM((NZ, ROWS, CH), BF),
            pltpu.VMEM((NC, CR, CH), BF),
            pltpu.VMEM((NC, CR // 2, CH), BF),
            pltpu.VMEM((NC, CR // 2, CH), BF),
            pltpu.VMEM((NC, CR, CH), BF),
            pltpu.VMEM((NC, CR, CH), BF),
            pltpu.VMEM((NC, CR, CH), BF),
            pltpu.VMEM((NC, CR, CH), BF),
            pltpu.VMEM((NC, 3, CR, CH), F32),
            dma((10,)),
            dma((NC,)),
            dma((2,)),
            dma((2, 7)), dma((2, 7)), dma((2,)),
            dma((2, 7)), dma((2, 7)), dma((2,)),
            dma((QS, 7)), dma((QS, 7)), dma((QS,)),
            dma((3, NY)), dma((3, NY)), dma((NY,)),
            dma((3,)), dma((3,)), dma((NY, 3)), dma((NY, 3)),
            dma((2, NC)), dma((2, NC)),
            dma((2, NC)), dma((2, NC)),
            dma((2, NC)), dma((2, NC)),
            dma((2, NC)), dma((2, NC)),
        ],
        compiler_params=pltpu.CompilerParams(
            collective_id=0, has_side_effects=True, vmem_limit_bytes=60 * 1024 * 1024
        ),
        name="hyena",
    )(streams, long_filter, conv_weight, skip_weight.reshape(1, CH), out_weight, *tables())


def solution(mesh):
    return jax.shard_map(
        on_device,
        mesh=mesh,
        in_specs=(
            P(None, "ctx", "tp"),
            P(None, None, "tp"),
            P("tp"),
            P("ctx", "tp"),
            P("tp", None),
        ),
        out_specs=P("ctx", "tp"),
        check_vma=False,
    )
```

time: 116 us -> 106 us (0.914)
  Pallas kernels: 114 us -> 104 us
    pallas_call x1, Pallas kernels: 114 us -> 104 us  [on_device(): pl.pallas_call(kernel, out_shape=jax.ShapeDtypeStruct((ROWS, CH), BF), in...]
where the time goes in v1:
time: 106 us
  Pallas kernels  104 us (98%)
  local copies, waits for them, and re-layouts  2.26 us (2%)
    pallas_call x1, Pallas kernels, on_device(): pl.pallas_call(kernel, out_shape=jax.ShapeDtypeStruct((ROWS, CH), BF), in...  104 us
    unnamed x1, local copies, waits for them, and re-layouts  2.26 us

profile of v1, /device:TPU:0, one launch (start us, length us, event | category | flops | bytes accessed | tf_op | source)
XLA Modules:
  0.0 105.8 jit_solution(4682615790698607490)
XLA Ops:
  0.0 103.5 %hyena.1 = bf16[1024,512]{1,0:T(8,128)(2,1)} custom-call(bf16[3,1024,512]{2,1,0:T(8,128)(2,1)} %x_ref.1, bf16[1024,512]{1,0:T(8,128)(2,1)} %h_ref.1, f32[3,3,512]{2,1,0:T(4,128)} %cw_ref.1, f32[1,512]{1,0:T(1,128)} %bitcast.1, bf16[512,8192]{1,0:T(8,128)(2,1)} %w_ref.1, bf16[512,256]{1,0:T(8,128)(2,1)} %constant.12.clone.f1_ref, ...), custom_call_target="tpu_custom_call" | custom-call | tf_op jit(solution)/shard_map/hyena/pallas_call | solution.py:407
  103.5 2.3 %copy.13 = bf16[1024,512]{1,0:T(8,128)(2,1)} copy(bf16[1024,512]{1,0:T(8,128)(2,1)} %hyena.1) | data formatting | bytes 2097152

commit v2 on v1

--- a/solution.py
+++ b/solution.py
@@ -27,6 +27,7 @@
 GROUPS = LC // 4
 NC = 8
 CR = ROWS // NC
+LINE = (2, 1)
 ORDER = (
     *"goowgofgfgofvmmorfrmofemoefrmrofmerfmermereree",
 )
@@ -119,8 +120,8 @@
     quarter = pl.multiple_of(half + (me // 2) * WQ, WQ)
     for d in (2, 1, 3):
         zp = (z + d) % NZ
-        first, count = (quarter, WQ) if d == 2 else (half, CH // 2)
         for k in range(NY):
+            first, count = (quarter, WQ) if d == 2 and k in LINE else (half, CH // 2)
             yb = (y + k) % NY
             cols = pl.multiple_of((NZ * yb + zp) * CH, CH)
             w_cps[d, k] = remote(
@@ -179,9 +180,9 @@
     for cp in h_cps[0] + h_cps[1]:
         cp.start()
 
-    for k, s in ((1, 1), (2, 2), (3, 0)):
+    for k in (1, 2):
         ins[k].wait()
-        x32[s, 8:, :] = xv[s].astype(F32)
+        x32[k, 8:, :] = xv[k].astype(F32)
     halo_cp.wait()
     edge = halo[...].astype(F32)[:, 8:16, :]
     x32[:, 0:8, :] = jnp.where(me == 0, jnp.zeros_like(edge), edge)
@@ -202,6 +203,9 @@
     for cp in u_cps[0] + u_cps[1]:
         cp.start()
 
+    ins[3].wait()
+    x32[0, 8:, :] = xv[0].astype(F32)
+
     for t in range(TILES):
         for q in range(CH // 256):
             gat[128 * t : 128 * t + 128, 256 * q : 256 * q + 256] = short(0, t, q)
@@ -234,8 +238,8 @@
     opp = pl.multiple_of(((z + 2) % NZ) * CH + quarter, WQ)
     x_cps = {}
 
-    def line(ks):
-        for k in ks:
+    def line():
+        for k in LINE:
             blk = wr.at[(y + k) % NY, pl.ds(opp, WQ), :]
             w_cps[2, k].wait()
             for n in range(1, 4):
@@ -258,7 +262,7 @@
         for cp in u_cps[h]:
             cp.wait()
         if h == 1:
-            line((2, 1))
+            line()
         r32[h] = ru[h].astype(F32).reshape(NA * LH, 128)
 
         def signal_pair(i, carry, h=h):
@@ -280,8 +284,6 @@
         cps.append(pltpu.make_async_copy(ys.at[q, me], ry.at[q, me], y_ls.at[q]))
         for cp in cps:
             cp.start()
-        if q == 0:
-            line((3, 0))
         y_cps.append(cps)
     eye128 = eye[0:128, 0:128]
 
@@ -309,6 +311,9 @@
                     w_cps[d, k].wait()
                 share(d)
         else:
+            for k in range(NY):
+                if k not in LINE:
+                    w_cps[2, k].wait()
             for cp in x_cps.values():
                 cp.wait()
             share(2)

time: 106 us -> 103 us (0.972)
  Pallas kernels: 104 us -> 101 us
    pallas_call x1, Pallas kernels: 104 us -> 101 us  [on_device(): pl.pallas_call(kernel, out_shape=jax.ShapeDtypeStruct((ROWS, CH), BF), in...]
where the time goes in v2:
time: 103 us
  Pallas kernels  101 us (98%)
  local copies, waits for them, and re-layouts  2.26 us (2%)
    pallas_call x1, Pallas kernels, on_device(): pl.pallas_call(kernel, out_shape=jax.ShapeDtypeStruct((ROWS, CH), BF), in...  101 us
    unnamed x1, local copies, waits for them, and re-layouts  2.26 us

profile of v2, /device:TPU:0, one launch (start us, length us, event | category | flops | bytes accessed | tf_op | source)
XLA Modules:
  0.0 103.0 jit_solution(17093970083461585942)
XLA Ops:
  0.0 100.7 %hyena.1 = bf16[1024,512]{1,0:T(8,128)(2,1)} custom-call(bf16[3,1024,512]{2,1,0:T(8,128)(2,1)} %x_ref.1, bf16[1024,512]{1,0:T(8,128)(2,1)} %h_ref.1, f32[3,3,512]{2,1,0:T(4,128)} %cw_ref.1, f32[1,512]{1,0:T(1,128)} %bitcast.1, bf16[512,8192]{1,0:T(8,128)(2,1)} %w_ref.1, bf16[512,256]{1,0:T(8,128)(2,1)} %constant.12.clone.f1_ref, ...), custom_call_target="tpu_custom_call" | custom-call | tf_op jit(solution)/shard_map/hyena/pallas_call | solution.py:412
  100.7 2.3 %copy.13 = bf16[1024,512]{1,0:T(8,128)(2,1)} copy(bf16[1024,512]{1,0:T(8,128)(2,1)} %hyena.1) | data formatting | bytes 2097152

commit v3 on v2

--- a/solution.py
+++ b/solution.py
@@ -306,17 +306,17 @@
 
     def weights(step):
         if step == 0:
-            for d in (1, 3):
-                for k in range(NY):
-                    w_cps[d, k].wait()
-                share(d)
-        else:
             for k in range(NY):
                 if k not in LINE:
                     w_cps[2, k].wait()
             for cp in x_cps.values():
                 cp.wait()
             share(2)
+            for d in (1, 3):
+                for k in range(NY):
+                    w_cps[d, k].wait()
+                share(d)
+        else:
             for cp in w_local:
                 cp.wait()
             for cp in f_cps.values():

time: 103 us -> 101 us (0.981)
  Pallas kernels: 101 us -> 97.9 us
    pallas_call x1, Pallas kernels: 101 us -> 97.9 us  [on_device(): pl.pallas_call(kernel, out_shape=jax.ShapeDtypeStruct((ROWS, CH), BF), in...]
where the time goes in v3:
time: 101 us; the launch traced here: 100 us
  Pallas kernels  97.9 us (97%)
  local copies, waits for them, and re-layouts  2.26 us (2%)
    pallas_call x1, Pallas kernels, on_device(): pl.pallas_call(kernel, out_shape=jax.ShapeDtypeStruct((ROWS, CH), BF), in...  97.9 us
    unnamed x1, local copies, waits for them, and re-layouts  2.26 us

profile of v3, /device:TPU:0, one launch (start us, length us, event | category | flops | bytes accessed | tf_op | source)
XLA Modules:
  0.0 100.1 jit_solution(10781090419408706725)
XLA Ops:
  0.0 97.9 %hyena.1 = bf16[1024,512]{1,0:T(8,128)(2,1)} custom-call(bf16[3,1024,512]{2,1,0:T(8,128)(2,1)} %x_ref.1, bf16[1024,512]{1,0:T(8,128)(2,1)} %h_ref.1, f32[3,3,512]{2,1,0:T(4,128)} %cw_ref.1, f32[1,512]{1,0:T(1,128)} %bitcast.1, bf16[512,8192]{1,0:T(8,128)(2,1)} %w_ref.1, bf16[512,256]{1,0:T(8,128)(2,1)} %constant.12.clone.f1_ref, ...), custom_call_target="tpu_custom_call" | custom-call | tf_op jit(solution)/shard_map/hyena/pallas_call | solution.py:412
  97.9 2.3 %copy.13 = bf16[1024,512]{1,0:T(8,128)(2,1)} copy(bf16[1024,512]{1,0:T(8,128)(2,1)} %hyena.1) | data formatting | bytes 2097152
